TPU v7x, 32 devices: a whole 2x2x4 slice. The times are simulated.
32 devices in a mesh: px: 8 (over y, x, core), py: 4 (over z).
Axes of the slice: x: 2, y: 2, z: 4, core: 2. Of those that a mesh axis runs over, the one named last changes fastest.
Arguments:
- nodes: bfloat16 [65536, 256], P(('px', 'py')), as said below
- w_query: bfloat16 [256, 256], replicated, may hold values from -0.375 to 0.375
- w_key: bfloat16 [256, 256], replicated, may hold values from -0.375 to 0.375
- w_value: bfloat16 [256, 256], replicated, may hold values from -0.375 to 0.375
- w_out: bfloat16 [256, 256], replicated, may hold values from -0.375 to 0.375
- omega: float32 [4, 64, 64], replicated, may hold values from -6 to 6
- hop_coef: float32 [2, 4], replicated, may hold values from 0.3 to 1
- ln_gain: float32 [256], replicated, may hold values from 0.5 to 1.5
- send_idx: int32 [32, 32, 16], P(('px', 'py')), may hold values from 0 to 2047
- send_count: int32 [32, 32], P(('px', 'py')), may hold values from 0 to 16, as said below
- tile_row: int32 [32, 20], P(('px', 'py')), may hold values from 0 to 15
- tile_col: int32 [32, 20], P(('px', 'py')), may hold values from 0 to 19, each once within a row
- tile_val: bfloat16 [32, 20, 128, 128], P(('px', 'py')), may hold values from -0.5 to 0.5
- grad_out: bfloat16 [65536, 256], P(('px', 'py')), may hold values from -6 to 6
Outputs:
- output: bfloat16 [65536, 256], P(('px', 'py'))
- grad_nodes: bfloat16 [65536, 256], P(('px', 'py'))
Inputs may be any that keep to these rules, and one draw needn't show every extreme that they name: `nodes`: node features. `send_idx`: a row of the sending partition's own 2048 nodes. `send_count`: slots at or beyond the count are padding; no partition sends to itself; every partition sends a full block of 16 rows to at least one other. `tile_col`: each partition's list names every column block once.
All inputs are finite; a program needn't handle non-finite values.
Results may differ from a plain program's by a relative error of at most 0.007.
Values may be sent and summed in bfloat16 or wider, within the bound.
A program may use at most 128 MiB of HBM per device.

v0:
```python
import jax
import jax.numpy as jnp
from jax import lax
from jax.sharding import PartitionSpec as P

H = 4
DH = 64
M = 64


EPSILON = 1e-05
HIGHEST = lax.Precision.HIGHEST


def project(rows_in, w_query, w_key, w_value):
    query = jnp.dot(rows_in, w_query, preferred_element_type=jnp.float32)
    keys = jnp.dot(rows_in, w_key, preferred_element_type=jnp.float32)
    values = jnp.dot(rows_in, w_value, preferred_element_type=jnp.float32)
    return (query, keys, values)


def features(source, omega):
    count = source.shape[0]
    heads = source.reshape(count, H, DH) * DH ** (-0.25)
    lifted = jnp.einsum("nhe,hem->nhm", heads, omega, precision=HIGHEST)
    return jnp.exp(lifted - 0.5 * jnp.sum(heads * heads, axis=2, keepdims=True)) * M ** (-0.5)


def key_summary(keys, values, omega):
    lifted = features(keys, omega)
    split_values = values.reshape(values.shape[0], H, DH)
    summary = jnp.einsum("nhm,nhe->hme", lifted, split_values, precision=HIGHEST)
    return (summary, jnp.sum(lifted, axis=0))


def attend(query, summary, normalizer, omega):
    lifted = features(query, omega)
    numerator = jnp.einsum("nhm,hme->nhe", lifted, summary, precision=HIGHEST)
    denominator = jnp.einsum("nhm,hm->nh", lifted, normalizer, precision=HIGHEST)
    return (numerator / denominator[:, :, None]).reshape(query.shape[0], H * DH)


def output_section(rows_in, mixed, w_out):
    total = rows_in.astype(jnp.float32) + jnp.dot(mixed, w_out, preferred_element_type=jnp.float32)
    centred = total - jnp.mean(total, axis=1, keepdims=True)
    inverse = lax.rsqrt(jnp.mean(centred * centred, axis=1, keepdims=True) + EPSILON)
    return (centred * inverse, inverse)


def norm_back(grad_rows, normed, inverse, ln_gain):
    scaled = grad_rows.astype(jnp.float32) * ln_gain
    return inverse * (
        scaled
        - jnp.mean(scaled, axis=1, keepdims=True)
        - normed * jnp.mean(scaled * normed, axis=1, keepdims=True)
    )


def spread(extended, tiles, tile_rows, tile_cols, row_blocks):
    tile = tiles.shape[-1]
    width = extended.shape[-1]
    blocks = extended.reshape(-1, tile, width)[tile_cols]
    products = jnp.einsum("tij,tjd->tid", tiles, blocks, preferred_element_type=jnp.float32)
    member = (tile_rows[None, :] == jnp.arange(row_blocks, dtype=jnp.int32)[:, None]).astype(
        jnp.float32
    )
    return jnp.einsum("bt,tid->bid", member, products, precision=HIGHEST).reshape(
        row_blocks * tile, width
    )


def collect(grads, tiles, tile_rows, tile_cols, col_blocks):
    tile = tiles.shape[-1]
    width = grads.shape[-1]
    blocks = grads.reshape(-1, tile, width)[tile_rows]
    products = jnp.einsum("tij,tid->tjd", tiles, blocks, preferred_element_type=jnp.float32)
    member = (tile_cols[None, :] == jnp.arange(col_blocks, dtype=jnp.int32)[:, None]).astype(
        jnp.float32
    )
    return jnp.einsum("bt,tjd->bjd", member, products, precision=HIGHEST).reshape(
        col_blocks * tile, width
    )


def deliver_rows(parcel):
    return lax.all_to_all(parcel, ("px", "py"), split_axis=0, concat_axis=0, tiled=True)


def return_grads(parcel):
    return lax.all_to_all(parcel, ("px", "py"), split_axis=0, concat_axis=0, tiled=True)


def shards(
    nodes,
    w_query,
    w_key,
    w_value,
    w_out,
    omega,
    hop_coef,
    ln_gain,
    send_idx,
    send_count,
    tile_row,
    tile_col,
    tile_val,
    grad_out,
):
    rows = nodes.shape[0]
    width = nodes.shape[1]
    tiles = tile_val[0]
    tile_rows = tile_row[0]
    tile_cols = tile_col[0]
    row_blocks = rows // tiles.shape[-1]
    col_blocks = tiles.shape[0]
    peers = send_idx.shape[1]
    slots = send_idx.shape[2]
    senders = send_idx[0].reshape(-1)
    live = (jnp.arange(slots, dtype=jnp.int32)[None, :] < send_count[0][:, None]).reshape(-1, 1)

    def relational_hop(source):
        outgoing = (source[senders] * live.astype(source.dtype)).reshape(peers, slots, width)
        incoming = deliver_rows(outgoing).reshape(peers * slots, width)
        extended = jnp.concatenate([source, incoming], axis=0)
        return spread(extended, tiles, tile_rows, tile_cols, row_blocks)

    def relational_back(grads):
        backward = collect(grads, tiles, tile_rows, tile_cols, col_blocks)
        remote = backward[rows:].astype(jnp.bfloat16).reshape(peers, slots, width)
        returned = return_grads(remote).reshape(peers * slots, width)
        added = (
            jnp.zeros((rows, width), jnp.float32)
            .at[senders]
            .add(returned.astype(jnp.float32) * live.astype(jnp.float32))
        )
        return backward[:rows] + added

    query, keys, values = project(nodes, w_query, w_key, w_value)
    local_summary, local_norm = key_summary(keys, values, omega)
    summary, normalizer = lax.psum((local_summary, local_norm), ("px", "py"))
    near = relational_hop(values.astype(jnp.bfloat16))
    far = relational_hop(near.astype(jnp.bfloat16))
    attention, pull = jax.vjp(
        lambda first_arg, second_arg, third_arg: attend(first_arg, second_arg, third_arg, omega),
        query,
        summary,
        normalizer,
    )
    hop_scale = jnp.repeat(hop_coef, DH, axis=1)
    mixed = (attention + hop_scale[0] * near + hop_scale[1] * far).astype(jnp.bfloat16)
    normed, inverse = output_section(nodes, mixed, w_out)
    output = (normed * ln_gain).astype(jnp.bfloat16)
    grad_total = norm_back(grad_out, normed, inverse, ln_gain)
    grad_mixed = jnp.dot(
        grad_total.astype(jnp.bfloat16), w_out.T, preferred_element_type=jnp.float32
    )
    grad_query, grad_summary, grad_norm = pull(grad_mixed)
    summary_total, norm_total = lax.psum((grad_summary, grad_norm), ("px", "py"))
    grad_far = (hop_scale[1] * grad_mixed).astype(jnp.bfloat16)
    grad_near = hop_scale[0] * grad_mixed + relational_back(grad_far)
    grad_hop = relational_back(grad_near.astype(jnp.bfloat16))
    _, pull_keys = jax.vjp(
        lambda first_arg, second_arg: key_summary(first_arg, second_arg, omega), keys, values
    )
    grad_keys, grad_values = pull_keys((summary_total, norm_total))
    grad_values = grad_values + grad_hop
    grad_nodes = grad_total + jnp.dot(
        grad_query.astype(jnp.bfloat16), w_query.T, preferred_element_type=jnp.float32
    )
    grad_nodes = grad_nodes + jnp.dot(
        grad_keys.astype(jnp.bfloat16), w_key.T, preferred_element_type=jnp.float32
    )
    grad_nodes = grad_nodes + jnp.dot(
        grad_values.astype(jnp.bfloat16), w_value.T, preferred_element_type=jnp.float32
    )
    return (output, grad_nodes.astype(jnp.bfloat16))


def solution(mesh):
    in_specs = (
        P(("px", "py"), None),
        P(),
        P(),
        P(),
        P(),
        P(),
        P(),
        P(),
        P(("px", "py"), None, None),
        P(("px", "py"), None),
        P(("px", "py"), None),
        P(("px", "py"), None),
        P(("px", "py"), None, None, None),
        P(("px", "py"), None),
    )
    out_specs = (P(("px", "py"), None), P(("px", "py"), None))
    return jax.shard_map(shards, mesh=mesh, in_specs=in_specs, out_specs=out_specs, check_vma=False)
```

profile of v0, /device:TPU:0, one launch (start us, length us, event | category | flops | bytes accessed | tf_op | source)
XLA Modules:
  0.0 389.0 jit_solution(11646883555022958842)
XLA Ops:
  7.2 3.2 broadcast_multiply_fusion.1
  13.2 2.3 fusion.38
  15.5 2.9 fusion.39
  18.7 2.3 copy.39
  21.6 2.9 gather_fusion
  25.4 7.3 %all-to-all-start = ((bf16[32,16,256]{2,1,0:T(8,128)(2,1)}), bf16[32,16,256]{2,1,0:T(8,128)(2,1)S(1)}, u32[]{:S(2)}, u32[]{:S(2)}) async-start(bf16[32,16,256]{2,1,0:T(8,128)(2,1)} %broadcast_multiply_fusion.3), calls=%async_computation | async-start | bytes 524288 | tf_op jit(solution)/shard_map/all_to_all | solution.py:86
  32.7 40.7 %psum.29 = f32[4,64]{1,0:T(4,128)S(1)} all-reduce(f32[4,64]{1,0:T(4,128)S(1)} %get-tuple-element.27), channel_id=1, replica_groups=mesh['px'=8,'py'=4] {'px','py'}, use_global_device_ids=true, to_apply=%region_4.0 | all-reduce | flops 256 | bytes 2048 | tf_op jit(solution)/shard_map/psum | solution.py:140
  73.4 3.2 broadcast_multiply_fusion
  76.6 2.0 fusion.94
  83.2 2.4 pad_maximum_fusion
  85.6 2.4 copy.41
  88.0 3.2 gather_fusion.1
  91.2 3.4 fusion.63
  94.6 3.5 copy.63
  98.1 3.2 fusion.6
  104.9 2.9 gather_fusion.2
  108.7 4.5 %all-to-all-start.1 = ((bf16[32,16,256]{2,1,0:T(8,128)(2,1)}), bf16[32,16,256]{2,1,0:T(8,128)(2,1)S(1)}, u32[]{:S(2)}, u32[]{:S(2)}) async-start(bf16[32,16,256]{2,1,0:T(8,128)(2,1)} %broadcast_multiply_fusion.2), calls=%async_computation.1 | async-start | bytes 524288 | tf_op jit(solution)/shard_map/all_to_all | solution.py:86
  113.8 2.3 copy.34
  116.4 2.3 copy.45
  118.7 27.5 %all-reduce.3.cloned.1.call-done = f32[4,64,64]{2,1,0:T(8,128)} async-done(((f32[4,64,64]{2,1,0:T(8,128)}), f32[4,64,64]{2,1,0:T(8,128)}) %all-reduce.3.cloned.1.call-update) | async-done | bytes 65552 | tf_op jit(solution)/shard_map/psum | solution.py:140
  146.2 5.8 %broadcast_divide_fusion.1 = (f32[2048,4,64]{0,2,1:T(8,128)}, f32[2048,4,64]{0,2,1:T(8,128)}) fusion(f32[2048,4]{0,1:T(4,128)S(1)} %bitcast.227, f32[4,64,64]{2,1,0:T(8,128)} %all-reduce.3.cloned.1.call-done, f32[4,2048,64]{1,2,0:T(8,128)} %copy-done.3, f32[2048,4]{0,1:T(4,128)S(1)} %get-tuple-element.18), kind=kOutput, calls=%fused_computation.86 | convolution fusion | flops 404226048 | bytes 6422528 | tf_op jit(solution)/shard_map/jvp(nhm,hme->nhe)/dot_general | solution.py:38
  152.0 2.9 copy.43
  154.9 2.4 pad_maximum_fusion.1
  157.3 3.2 gather_fusion.3
  160.5 3.4 fusion.61
  163.9 3.5 copy.64
  167.3 3.2 fusion.4
  174.8 1.7 copy-done.12
  176.5 1.6 fusion.33
  178.1 2.7 multiply_convert_fusion
  180.8 3.0 copy.46
  183.9 2.9 multiply_reduce_fusion
  187.4 3.1 fusion.20
  190.5 5.0 %fusion.19 = (f32[2048,4]{0,1:T(4,128)S(1)}, f32[4,2048,64]{1,2,0:T(8,128)S(1)}) fusion(f32[4,2048,64]{1,2,0:T(8,128)} %copy-done.3, f32[2048,4]{0,1:T(4,128)S(1)} %get-tuple-element.18, f32[4,64,64]{2,1,0:T(8,128)S(1)} %copy-done.41, f32[2048,4,64]{0,2,1:T(8,128)} %bitcast.211, f32[2048,4]{0,1:T(4,128)S(1)} %bitcast.229, f32[4,64]{1,0:T(4,128)S(1)} %psum.29, ...), kind=kOutput, calls=%fused_computation.40 | convolution fusion | flops 406315008 | bytes 6489088 | tf_op jit(solution)/shard_map/transpose(jvp(nhm,hme->nhe))/dot_general | solution.py:38
  195.6 2.4 fusion.16
  198.1 2.2 convolution_add_fusion.3
  200.2 3.0 gather_fusion.4
  203.2 3.4 fusion.59
  206.6 3.5 copy.70
  210.1 3.6 fusion.2
  215.6 1.6 bitcast_add_fusion.1
  217.9 2.0 fusion.52
  220.7 3.6 all-to-all-start.2
  224.3 2.3 copy.56
  226.6 40.7 %psum.30 = f32[4,64]{1,0:T(4,128)S(1)} all-reduce(f32[4,64]{1,0:T(4,128)S(1)} %bitcast.231), channel_id=1, replica_groups=mesh['px'=8,'py'=4] {'px','py'}, use_global_device_ids=true, to_apply=%region_11.0 | all-reduce | flops 256 | bytes 2048 | tf_op jit(solution)/shard_map/psum | solution.py:158
  267.3 46.9 %all-reduce.5.cloned.1.call-done = f32[4,64,64]{2,1,0:T(8,128)} async-done(((f32[4,64,64]{2,1,0:T(8,128)}), f32[4,64,64]{2,1,0:T(8,128)}) %all-reduce.5.cloned.1.call-update) | async-done | bytes 65552 | tf_op jit(solution)/shard_map/psum | solution.py:158
  314.2 5.3 %fusion.18 = (f32[2048,4]{0,1:T(4,128)S(1)}, f32[4,64,2048]{2,1,0:T(8,128)}) fusion(f32[4,2048,64]{1,2,0:T(8,128)S(1)} %get-tuple-element.28, f32[2048,4]{0,1:T(4,128)S(1)} %get-tuple-element.14, f32[4,64,64]{2,1,0:T(8,128)} %all-reduce.5.cloned.1.call-done, f32[2048,4,64]{0,2,1:T(8,128)} %bitcast.206, f32[4,64]{1,0:T(4,128)S(1)} %psum.30), kind=kOutput, calls=%fused_computation.38 | convolution fusion | flops 405266432 | bytes 6423552 | tf_op jit(solution)/shard_map/transpose(jvp(nhm,nhe->hme))/dot_general | solution.py:32
  319.5 3.4 fusion.36
  322.9 3.0 copy.53
  325.9 5.6 %fusion.17 = bf16[2048,4,64]{0,2,1:T(8,128)(2,1)} fusion(f32[4,64,64]{2,1,0:T(8,128)S(1)} %copy-done.21, f32[4,64,2048]{2,1,0:T(8,128)} %get-tuple-element.38, f32[2048,4,64]{0,2,1:T(8,128)} %bitcast.207, f32[4,2048,64]{1,2,0:T(8,128)S(1)} %get-tuple-element.28, f32[4,2048]{1,0:T(4,128)S(1)} %get-tuple-element.13, f32[2048,4]{0,1:T(4,128)S(1)} %negate_multiply_fusion), kind=kOutput, calls=%fused_computation.33 | convolution fusion | flops 405798912 | bytes 7471104 | tf_op jit(solution)/shard_map/transpose(jvp(nhe,hem->nhm))/dot_general | solution.py:25
  331.5 6.2 %scatter_custom_fusion = f32[2048,256]{1,0:T(8,128)} fusion(f32[2048,256]{1,0:T(8,128)} %bitcast_add_fusion.1, s32[512]{0:T(512)} %bitcast.233, bf16[512,256]{1,0:T(8,128)(2,1)S(1)} %bitcast.223, f32[512]{0:T(512)S(1)} %reshape.269), kind=kCustom, calls=%fused_computation.106 | custom fusion | flops 393216 | bytes 2361344 | tf_op jit(solution)/shard_map/scatter-add | solution.py:134
  337.7 1.7 convert_element_type.110
  339.4 1.8 gather_fusion.5
  341.1 3.4 fusion.57
  344.5 3.7 copy.71
  348.2 3.6 fusion
  352.2 2.5 copy.52
  355.4 3.6 all-to-all-start.3
  359.1 3.2 bitcast_add_fusion
  362.3 7.0 %all-to-all-done.3 = bf16[32,16,256]{2,1,0:T(8,128)(2,1)S(1)} async-done(((bf16[32,16,256]{2,1,0:T(8,128)(2,1)}), bf16[32,16,256]{2,1,0:T(8,128)(2,1)S(1)}, u32[]{:S(2)}, u32[]{:S(2)}) %all-to-all-start.3) | async-done | bytes 262176 | tf_op jit(solution)/shard_map/all_to_all | solution.py:90
  369.3 6.2 %scatter_custom_fusion.1 = f32[2048,256]{1,0:T(8,128)} fusion(f32[2048,256]{1,0:T(8,128)} %bitcast_add_fusion, s32[512]{0:T(512)} %bitcast.234, bf16[512,256]{1,0:T(8,128)(2,1)S(1)} %bitcast.224, f32[512]{0:T(512)S(1)} %reshape.269), kind=kCustom, calls=%fused_computation.104 | custom fusion | flops 393216 | bytes 2361344 | tf_op jit(solution)/shard_map/scatter-add | solution.py:134
  375.5 2.2 fusion.41
  377.9 1.5 fusion.15
  379.5 2.3 copy.57
  (135 shorter events, 24.0 us)
Async XLA Ops:
  7.2 84.1 %copy-start = (bf16[1,20,128,128]{3,2,1,0:T(8,128)(2,1)S(1)}, bf16[1,20,128,128]{3,2,1,0:T(8,128)(2,1)}, u32[]{:S(2)}) copy-start(bf16[1,20,128,128]{3,2,1,0:T(8,128)(2,1)} %param.26) | copy-start | bytes 1966084
  7.2 139.1 %all-reduce.3.cloned.1.call-start = ((), (), s32[]{:S(2)}) async-start(), calls=%async_computation.4 | async-start | bytes 262144 | tf_op jit(solution)/shard_map/psum | solution.py:140
  10.5 1.2 copy-start.11
  10.5 1.2 copy-start.25
  11.7 1.5 copy-start.21
  13.2 2.3 copy-start.7
  15.5 3.0 copy-start.32
  18.4 2.5 copy-start.40
  18.6 2.3 copy-start.33
  25.4 57.7 %all-to-all-start = ((bf16[32,16,256]{2,1,0:T(8,128)(2,1)}), bf16[32,16,256]{2,1,0:T(8,128)(2,1)S(1)}, u32[]{:S(2)}, u32[]{:S(2)}) async-start(bf16[32,16,256]{2,1,0:T(8,128)(2,1)} %broadcast_multiply_fusion.3), calls=%async_computation | async-start | bytes 524288 | tf_op jit(solution)/shard_map/all_to_all | solution.py:86
  78.6 3.2 copy-start.3
  78.6 1.2 copy-start.34
  78.6 1.2 copy-start.39
  94.6 3.5 copy-start.38
  102.5 1.3 copy-start.9
  107.9 8.2 %copy-start.37 = (f32[4]{0:T(128)S(1)}, f32[4]{0:T(128)}, u32[]{:S(2)}) copy-start(f32[4]{0:T(128)} %get-tuple-element.19) | copy-start | bytes 52
  107.9 8.4 %copy-start.36 = (f32[4]{0:T(128)S(1)}, f32[4]{0:T(128)}, u32[]{:S(2)}) copy-start(f32[4]{0:T(128)} %get-tuple-element.20) | copy-start | bytes 52
  108.7 46.2 %all-to-all-start.1 = ((bf16[32,16,256]{2,1,0:T(8,128)(2,1)}), bf16[32,16,256]{2,1,0:T(8,128)(2,1)S(1)}, u32[]{:S(2)}, u32[]{:S(2)}) async-start(bf16[32,16,256]{2,1,0:T(8,128)(2,1)} %broadcast_multiply_fusion.2), calls=%async_computation.1 | async-start | bytes 524288 | tf_op jit(solution)/shard_map/all_to_all | solution.py:86
  113.3 200.9 %all-reduce.5.cloned.1.call-start = ((), (), s32[]{:S(2)}) async-start(), calls=%async_computation.5 | async-start | bytes 262144 | tf_op jit(solution)/shard_map/psum | solution.py:158
  113.8 4.9 %copy-start.30 = (f32[32,16]{1,0:T(8,128)S(1)}, f32[32,16]{1,0:T(8,128)}, u32[]{:S(2)}) copy-start(f32[32,16]{1,0:T(8,128)} %get-tuple-element.21) | copy-start | bytes 6148
  170.6 1.6 copy-start.10
  170.6 2.2 copy-start.18
  172.8 1.2 copy-start.20
  172.8 1.2 copy-start.24
  174.5 3.6 copy-start.1
  174.5 2.0 copy-start.12
  174.5 2.0 copy-start.31
  180.8 3.0 copy-start.29
  183.9 2.9 copy-start.4
  183.9 3.5 copy-start.17
  187.4 3.1 copy-start.41
  190.5 5.1 %copy-start.5 = (f32[4,2048,64]{1,2,0:T(8,128)S(1)}, f32[4,2048,64]{1,2,0:T(8,128)}, u32[]{:S(2)}) copy-start(f32[4,2048,64]{1,2,0:T(8,128)} %copy-done.3) | copy-start | bytes 6291460
  190.5 5.1 %copy-start.14 = (f32[2048,256]{0,1:T(8,128)S(1)}, f32[2048,256]{0,1:T(8,128)}, u32[]{:S(2)}) copy-start(f32[2048,256]{0,1:T(8,128)} %get-tuple-element.9) | copy-start | bytes 6291460
  190.5 5.1 %copy-start.28 = (f32[4,2048]{1,0:T(4,128)S(1)}, f32[4,2048]{1,0:T(4,128)}, u32[]{:S(2)}) copy-start(f32[4,2048]{1,0:T(4,128)} %get-tuple-element.17) | copy-start | bytes 98308
  195.6 2.5 copy-start.2
  195.6 2.5 copy-start.13
  195.6 2.4 copy-start.22
  206.6 3.5 copy-start.35
  213.9 1.6 copy-start.8
  215.5 2.4 copy-start.6
  220.7 110.8 %all-to-all-start.2 = ((bf16[32,16,256]{2,1,0:T(8,128)(2,1)}), bf16[32,16,256]{2,1,0:T(8,128)(2,1)S(1)}, u32[]{:S(2)}, u32[]{:S(2)}) async-start(bf16[32,16,256]{2,1,0:T(8,128)(2,1)} %bitcast.57), calls=%async_computation.2 | async-start | bytes 524288 | tf_op jit(solution)/shard_map/all_to_all | solution.py:90
  314.2 5.3 %copy-start.27 = (f32[4,64,64]{2,1,0:T(8,128)S(1)}, f32[4,64,64]{2,1,0:T(8,128)}, u32[]{:S(2)}) copy-start(f32[4,64,64]{2,1,0:T(8,128)} %all-reduce.5.cloned.1.call-done) | copy-start | bytes 196612
  352.2 6.9 %copy-start.16 = (f32[2048,256]{1,0:T(8,128)S(1)}, f32[2048,256]{1,0:T(8,128)}, u32[]{:S(2)}) copy-start(f32[2048,256]{1,0:T(8,128)} %copy.53) | copy-start | bytes 6291460
  355.4 13.9 %all-to-all-start.3 = ((bf16[32,16,256]{2,1,0:T(8,128)(2,1)}), bf16[32,16,256]{2,1,0:T(8,128)(2,1)S(1)}, u32[]{:S(2)}, u32[]{:S(2)}) async-start(bf16[32,16,256]{2,1,0:T(8,128)(2,1)} %bitcast.62), calls=%async_computation.3 | async-start | bytes 524288 | tf_op jit(solution)/shard_map/all_to_all | solution.py:90
  362.3 13.2 %copy-start.26 = (bf16[256,256]{1,0:T(8,128)(2,1)S(1)}, bf16[256,256]{1,0:T(8,128)(2,1)}, u32[]{:S(2)}) copy-start(bf16[256,256]{1,0:T(8,128)(2,1)} %param.17) | copy-start | bytes 393220
  375.5 2.2 copy-start.15
  375.5 2.5 copy-start.19
  375.5 2.5 copy-start.23
Sparse Core Ops, SparseCore 0:
  18.6 127.6 all-reduce.2
  190.6 123.5 all-reduce.4
where the time goes:
time: 396 us; the launch traced here: 389 us
  matrix products  85.2 us (22%)
  waiting for transfers between devices  81.5 us (21%)
  blocking collectives  81.4 us (21%)
  local copies, waits for them, and re-layouts  71.2 us (18%)
  other arithmetic  35 us (9%)
  starting transfers between devices  19.6 us (5%)
  between operations  15.1 us (4%)
    psum x1, waiting for transfers between devices, shards(): lax.psum((grad_summary, grad_norm), ('px', 'py'))  46.9 us
    psum x1, blocking collectives, shards(): summary, normalizer = lax.psum((local_summary, local_norm), ('px', 'py'))  40.7 us
    psum x1, blocking collectives, shards(): lax.psum((grad_summary, grad_norm), ('px', 'py'))  40.7 us
    psum x1, waiting for transfers between devices, shards(): summary, normalizer = lax.psum((local_summary, local_norm), ('px', 'py'))  27.5 us
    unnamed x89, local copies, waits for them, and re-layouts  16.9 us
    dot_general x3, matrix products, attend(): numerator = jnp.einsum('nhm,hme->nhe', lifted, summary, precision=HIGHEST)  13.8 us
    scatter-add x2, other arithmetic, relational_back(): added = jnp.zeros((rows, width), jnp.float32).at[senders].add(returned.as...  12.3 us
    dot_general x4, matrix products, features(): lifted = jnp.einsum('nhe,hem->nhm', heads, omega, precision=HIGHEST)  12.3 us
  transfers between devices with their start and end apart: 6, of which 3 were waited for; matrix products, arithmetic and copies ran while one was open for 27% of the time, Pallas kernels for 0%

commit v1 on v0

v1 whole, which is shorter than its diff:
```python
import functools

import jax
import jax.numpy as jnp
from jax import lax
from jax.experimental import pallas as pl
from jax.experimental.pallas import tpu as pltpu
from jax.sharding import PartitionSpec as P

EPSILON = 1e-05
F32 = jnp.float32
BF16 = jnp.bfloat16
EXTRA = 8
BLOCK = 256
NN = (((1,), (0,)), ((), ()))
NT = (((1,), (1,)), ((), ()))
TN = (((0,), (0,)), ((), ()))


def mm(a, b, dims=NN):
    return lax.dot_general(a, b, dims, preferred_element_type=F32)


def split(x):
    high = x.astype(BF16)
    return high, (x - high.astype(F32)).astype(BF16)


def mm3(x, w, dims=NN):
    xh, xl = x
    wh, wl = w
    return mm(xh, wh, dims) + (mm(xl, wh, dims) + mm(xh, wl, dims))


def mm2(x, w, dims=NN):
    xh, xl = x
    return mm(xh, w, dims) + mm(xl, w, dims)


def iota(shape, axis):
    return lax.broadcasted_iota(jnp.int32, shape, axis)


def ones_where(mask):
    return jnp.where(mask, 1.0, 0.0).astype(BF16)


def head_mask(width, head):
    return iota((width, width), 0) // head == iota((width, width), 1) // head


def features(u, omega, ones, head):
    square = mm2(split(u * u), ones)
    return jnp.exp(mm3(split(u), omega) - square * (0.5 * head**-0.5)) * head**-0.5


def features_back(grad, phi, u, omega, ones, head):
    arg = split(grad * phi)
    return mm3(arg, omega, NT) - u * (mm2(arg, ones) * head**-0.5)


def gather_rows(idx_ref, src_ref, pay_ref, slots):
    rows, width = src_ref.shape
    group = 128 // slots

    def step(i, c):
        start = pl.multiple_of(i * 128, 128)
        wanted = idx_ref[pl.ds(start, 128), :]
        picked = mm(ones_where(iota((128, rows), 1) == wanted), src_ref[...])
        pay_ref[pl.ds(i * group, group), 0:slots, :] = picked.astype(BF16).reshape(
            group, slots, width
        )
        return c

    lax.fori_loop(0, idx_ref.shape[0] // 128, step, 0)


def scatter_rows(idx_row, received, start, count):
    slots_all = received.shape[0]
    hit = ones_where(iota((count, slots_all), 0) + start == idx_row)
    return mm(hit, received)


def pack_sums(pay_ref, slots, total, norm, head, per):
    peers, _, width = pay_ref.shape
    kept = jnp.where(head_mask(width, head), total, 0.0)
    folded = kept[0:head]
    for h in range(1, width // head):
        folded = folded + kept[h * head : (h + 1) * head]
    high, low = split(folded)
    nh, nl = split(norm)
    r, m = iota((peers * EXTRA, head), 0), iota((peers * EXTRA, head), 1)
    owner = m // per == r // EXTRA
    slot = r % EXTRA
    out = mm(ones_where(owner & (slot == m % per)), high)
    out = out + mm(ones_where(owner & (slot == m % per + per)), low)
    k = iota((peers * EXTRA, width), 0) % EXTRA
    out = out + jnp.where(k == EXTRA - 2, nh.astype(F32), 0.0)
    out = out + jnp.where(k == EXTRA - 1, nl.astype(F32), 0.0)
    pay_ref[:, slots : slots + EXTRA, :] = out.reshape(peers, EXTRA, width).astype(BF16)


def relay_sums(rec_ref, pay_ref, slots, norm_ref, per):
    peers, _, width = rec_ref.shape
    s8 = jnp.sum(rec_ref[:, slots : slots + EXTRA, :].astype(F32), axis=0)
    norm = s8[EXTRA - 2 : EXTRA - 1] + s8[EXTRA - 1 : EXTRA]
    norm_ref[...] = jnp.broadcast_to(norm, (8, width))
    k = iota((EXTRA, width), 0)
    own = s8 + pltpu.roll(s8, EXTRA - per, 0)
    high = own.astype(BF16).astype(F32)
    low = pltpu.roll(own - high, per, 0)
    out = jnp.where(k < per, high, jnp.where(k < 2 * per, low, 0.0))
    pay_ref[:, slots : slots + EXTRA, :] = jnp.broadcast_to(
        out[None], (peers, EXTRA, width)
    ).astype(BF16)


def unpack_sums(rec_ref, slots, head, per):
    peers, _, width = rec_ref.shape
    sent = rec_ref[:, slots : slots + EXTRA, :].astype(F32).reshape(peers * EXTRA, width)
    sent = sent.astype(BF16)
    m, r = iota((head, peers * EXTRA), 0), iota((head, peers * EXTRA), 1)
    owner = m // per == r // EXTRA
    slot = r % EXTRA
    mask = head_mask(width, head)
    out = []
    for at in (m % per, m % per + per):
        piece = mm(ones_where(owner & (slot == at)), sent)
        full = jnp.concatenate([piece] * (width // head), axis=0)
        out.append(jnp.where(mask, full, 0.0).astype(BF16))
    return tuple(out)


def spread(row_ref, col_ref, tiles_ref, src_ref, rec_ref, slots, out_ref):
    rows, width = src_ref.shape
    tile = tiles_ref.shape[1]
    group = tile // slots
    own = rows // tile
    out_ref[...] = jnp.zeros_like(out_ref)
    peers = rec_ref.shape[0]

    def step(t, c):
        block = col_ref[0, t]
        at = pl.multiple_of(row_ref[0, t] * tile, tile)
        first = pl.multiple_of(jnp.minimum(block, own - 1) * tile, tile)
        far = jnp.clip(block - own, 0, peers // group - 1) * group
        mine = src_ref[pl.ds(first, tile), :]
        theirs = rec_ref[pl.ds(far, group), 0:slots, :].reshape(tile, width)
        picked = jnp.where(block < own, mine, theirs)
        out_ref[pl.ds(at, tile), :] += mm(tiles_ref[t], picked)
        return c

    lax.fori_loop(0, tiles_ref.shape[0], step, 0, unroll=4)


def collect(row_ref, col_ref, tiles_ref, src_ref, pay_ref, slots, local_ref):
    rows, width = src_ref.shape
    tile = tiles_ref.shape[1]
    group = tile // slots
    own = rows // tile

    def step(t, c):
        block = col_ref[0, t]
        at = pl.multiple_of(row_ref[0, t] * tile, tile)
        product = mm(tiles_ref[t], src_ref[pl.ds(at, tile), :], TN)

        @pl.when(block < own)
        def _():
            local_ref[pl.ds(pl.multiple_of(block * tile, tile), tile), :] = product

        @pl.when(block >= own)
        def _():
            pay_ref[pl.ds((block - own) * group, group), 0:slots, :] = product.astype(
                BF16
            ).reshape(group, slots, width)

        return c

    lax.fori_loop(0, tiles_ref.shape[0], step, 0, unroll=4)


def over_blocks(rows, step):
    def run(i, c):
        step(pl.multiple_of(i * BLOCK, BLOCK))
        return c

    lax.fori_loop(0, rows // BLOCK, run, 0)


def first_kernel(dims, idx, nodes, w_key, w_value, omega, values_b, pay, total, norm):
    head, slots, per = dims
    width = nodes.shape[1]
    ones = ones_where(head_mask(width, head))
    om = split(omega[...])
    total[...] = jnp.zeros_like(total)
    norm[...] = jnp.zeros_like(norm)

    def step(at):
        x = nodes[pl.ds(at, BLOCK), :]
        keys = mm(x, w_key[...])
        values = mm(x, w_value[...])
        phi = features(keys, om, ones, head)
        values_b[pl.ds(at, BLOCK), :] = values.astype(BF16)
        total[...] += mm3(split(phi), split(values), TN)
        norm[...] += jnp.sum(phi, axis=0, keepdims=True)

    over_blocks(nodes.shape[0], step)
    gather_rows(idx, values_b, pay, slots)
    pack_sums(pay, slots, total[...], norm[...], head, per)


def second_kernel(dims, row, col, idx, values_b, rec, tiles, near_b, pay, norm, near):
    head, slots, per = dims
    relay_sums(rec, pay, slots, norm, per)
    spread(row, col, tiles, values_b, rec, slots, near)

    def step(at):
        near_b[pl.ds(at, BLOCK), :] = near[pl.ds(at, BLOCK), :].astype(BF16)

    over_blocks(near.shape[0], step)
    gather_rows(idx, near_b, pay, slots)


def third_kernel(
    dims, row, col, coef, nodes, grad_out, near_b, rec, norm, tiles, w_query, w_out, omega, gain,
    output, partial, grad_near, pay, far, grad_far, total, dnorm, local,
):
    head, slots, per = dims
    rows, width = nodes.shape
    ones = ones_where(head_mask(width, head))
    om = split(omega[...])
    summary = unpack_sums(rec, slots, head, per)
    z = norm[0:1, :]
    lane_head = iota((1, width), 1) // head
    near_scale = jnp.zeros((1, width), F32)
    far_scale = jnp.zeros((1, width), F32)
    for h in range(width // head):
        near_scale = jnp.where(lane_head == h, coef[0, h], near_scale)
        far_scale = jnp.where(lane_head == h, coef[1, h], far_scale)
    spread(row, col, tiles, near_b, rec, slots, far)
    total[...] = jnp.zeros_like(total)
    dnorm[...] = jnp.zeros_like(dnorm)

    def step(at):
        here = pl.ds(at, BLOCK)
        x = nodes[here, :]
        query = mm(x, w_query[...])
        phi = features(query, om, ones, head)
        phis = split(phi)
        inv_den = 1.0 / mm2(split(phi * z), ones)
        attention = mm3(phis, summary) * inv_den
        mixed = attention + near_scale * near_b[here, :].astype(F32) + far_scale * far[here, :]
        whole = x.astype(F32) + mm(mixed.astype(BF16), w_out[...])
        centred = whole - jnp.mean(whole, axis=1, keepdims=True)
        inverse = lax.rsqrt(jnp.mean(centred * centred, axis=1, keepdims=True) + EPSILON)
        normed = centred * inverse
        output[here, :] = (normed * gain[...]).astype(BF16)
        g = grad_out[here, :].astype(F32) * gain[...]
        grad_total = inverse * (
            g
            - jnp.mean(g, axis=1, keepdims=True)
            - normed * jnp.mean(g * normed, axis=1, keepdims=True)
        )
        grad_mixed = mm(grad_total.astype(BF16), w_out[...], NT)
        grad_far[here, :] = (far_scale * grad_mixed).astype(BF16)
        grad_near[here, :] = near_scale * grad_mixed
        a = grad_mixed * inv_den
        pulls = split(a)
        r = mm2(split(a * attention), ones)
        grad_phi = mm3(pulls, summary, NT) - r * z
        total[...] += mm3(phis, pulls, TN)
        dnorm[...] -= jnp.sum(phi * r, axis=0, keepdims=True)
        grad_query = features_back(grad_phi, phi, query, om, ones, head)
        partial[here, :] = grad_total + mm(grad_query.astype(BF16), w_query[...], NT)

    over_blocks(rows, step)
    collect(row, col, tiles, grad_far, pay, slots, local)

    def add(at):
        here = pl.ds(at, BLOCK)
        grad_near[here, :] += local[here, :]

    over_blocks(rows, add)
    pack_sums(pay, slots, total[...], dnorm[...], head, per)


def fourth_kernel(dims, row, col, idx_row, grad_near, rec, tiles, grad_hop, pay, norm, near_b):
    head, slots, per = dims
    peers, _, width = rec.shape
    relay_sums(rec, pay, slots, norm, per)
    returned = rec[:, 0:slots, :].reshape(peers * slots, width)
    wanted = idx_row[...]

    def step(at):
        here = pl.ds(at, BLOCK)
        added = scatter_rows(wanted, returned, at, BLOCK)
        near_b[here, :] = (grad_near[here, :] + added).astype(BF16)

    over_blocks(near_b.shape[0], step)
    collect(row, col, tiles, near_b, pay, slots, grad_hop)


def fifth_kernel(
    dims, idx_row, nodes, partial, grad_hop, rec, norm, w_key, w_value, omega, grad_nodes
):
    head, slots, per = dims
    peers, _, width = rec.shape
    ones = ones_where(head_mask(width, head))
    om = split(omega[...])
    summary = unpack_sums(rec, slots, head, per)
    z = norm[0:1, :]
    returned = rec[:, 0:slots, :].reshape(peers * slots, width)
    wanted = idx_row[...]

    def step(at):
        here = pl.ds(at, BLOCK)
        x = nodes[here, :]
        keys = mm(x, w_key[...])
        values = mm(x, w_value[...])
        phi = features(keys, om, ones, head)
        grad_phi = mm3(split(values), summary, NT) + z
        added = scatter_rows(wanted, returned, at, BLOCK)
        grad_values = mm3(split(phi), summary) + (grad_hop[here, :] + added)
        grad_keys = features_back(grad_phi, phi, keys, om, ones, head)
        out = partial[here, :] + mm(grad_keys.astype(BF16), w_key[...], NT)
        out = out + mm(grad_values.astype(BF16), w_value[...], NT)
        grad_nodes[here, :] = out.astype(BF16)

    over_blocks(nodes.shape[0], step)


def call(body, dims, name, smem, outs, scratch, *args):
    vm = pl.BlockSpec(memory_space=pltpu.VMEM)
    sm = pl.BlockSpec(memory_space=pltpu.SMEM)
    return pl.pallas_call(
        functools.partial(body, dims),
        in_specs=[sm] * smem + [vm] * (len(args) - smem),
        out_specs=[vm] * len(outs),
        out_shape=[jax.ShapeDtypeStruct(s, t) for s, t in outs],
        scratch_shapes=[pltpu.VMEM(s, t) for s, t in scratch],
        name=name,
    )(*args)


def exchange(parcel):
    return lax.all_to_all(parcel, ("px", "py"), split_axis=0, concat_axis=0, tiled=True)


def shards(
    nodes, w_query, w_key, w_value, w_out, omega, hop_coef, ln_gain,
    send_idx, send_count, tile_row, tile_col, tile_val, grad_out,
):
    rows, width = nodes.shape
    heads, head, _ = omega.shape
    tiles = tile_val[0]
    peers, slots = send_idx.shape[1:]
    per = -(-head // peers)
    assert 2 * per <= EXTRA - 2
    dims = (head, slots, per)
    live = jnp.arange(slots, dtype=jnp.int32)[None, :] < send_count[0][:, None]
    idx = jnp.where(live, send_idx[0], -1)
    idx_row = idx.reshape(1, peers * slots)
    idx_col = idx.reshape(peers * slots, 1)
    lane = jnp.arange(width, dtype=jnp.int32) // head
    wide = jnp.tile(omega.reshape(width, head), (1, heads)) * head**-0.25
    wide = jnp.where(lane[:, None] == lane[None, :], wide, 0.0)
    gain = ln_gain.reshape(1, width)
    full_b, full_f = ((rows, width), BF16), ((rows, width), F32)
    pay = ((peers, slots + EXTRA, width), BF16)
    norm = ((8, width), F32)
    sums, row = ((width, width), F32), ((1, width), F32)

    values_b, sent = call(
        first_kernel, dims, "keys", 0, [full_b, pay], [sums, row],
        idx_col, nodes, w_key, w_value, wide,
    )
    got = exchange(sent)
    near_b, sent, z = call(
        second_kernel, dims, "near", 2, [full_b, pay, norm], [full_f],
        tile_row, tile_col, idx_col, values_b, got, tiles,
    )
    got = exchange(sent)
    output, partial, grad_near, sent = call(
        third_kernel, dims, "middle", 3, [full_b, full_f, full_f, pay],
        [full_f, full_b, sums, row, full_f],
        tile_row, tile_col, hop_coef, nodes, grad_out, near_b, got, z, tiles,
        w_query, w_out, wide, gain,
    )
    got = exchange(sent)
    grad_hop, sent, dz = call(
        fourth_kernel, dims, "back", 2, [full_f, pay, norm], [full_b],
        tile_row, tile_col, idx_row, grad_near, got, tiles,
    )
    got = exchange(sent)
    (grad_nodes,) = call(
        fifth_kernel, dims, "last", 0, [full_b], [],
        idx_row, nodes, partial, grad_hop, got, dz, w_key, w_value, wide,
    )
    return output, grad_nodes


def solution(mesh):
    both = ("px", "py")
    in_specs = (
        P(both, None), P(), P(), P(), P(), P(), P(), P(),
        P(both, None, None), P(both, None), P(both, None), P(both, None),
        P(both, None, None, None), P(both, None),
    )
    out_specs = (P(both, None), P(both, None))
    return jax.shard_map(shards, mesh=mesh, in_specs=in_specs, out_specs=out_specs, check_vma=False)
```

time: 396 us -> 140 us (0.35); the launches traced: 389 us -> 139 us
  matrix products: 85.2 us -> 0 us
  waiting for transfers between devices: 81.5 us -> 11.1 us
  local copies, waits for them, and re-layouts: 71.2 us -> 2.25 us
  Pallas kernels: 0 us -> 66.3 us
  other arithmetic: 35 us -> 3.8 us
  blocking collectives: 81.4 us -> 50.8 us
  starting transfers between devices: 19.6 us -> 3.82 us
  between operations: 15.1 us -> 0.7 us
    dot_general x28 -> x0, matrix products: 85.2 us -> none  [the longest x3 13.8 us: attend(): numerator = jnp.einsum('nhm,hme->nhe', lifted, summary, precision=HIGHEST)]
    psum x2 -> x0, blocking collectives: 81.4 us -> none  [the longest x1 40.7 us: shards(): summary, normalizer = lax.psum((local_summary, local_norm), ('px', 'py'))]
    psum x2 -> x0, waiting for transfers between devices: 74.4 us -> none  [the longest x1 46.9 us: shards(): lax.psum((grad_summary, grad_norm), ('px', 'py'))]
    pallas_call x0 -> x5, Pallas kernels: none -> 66.3 us  [call(): pl.pallas_call(functools.partial(body, dims), in_specs=[sm] * smem + [vm]...]
    all_to_all x0 -> x3, blocking collectives: none -> 50.8 us  [exchange(): lax.all_to_all(parcel, ('px', 'py'), split_axis=0, concat_axis=0, tiled=T...]
    dot_general x8 -> x0, local copies, waits for them, and re-layouts: 19.6 us -> none  [the longest x2 7.17 us: collect(): jnp.einsum('tij,tid->tjd', tiles, blocks, preferred_element_type=jnp.floa...]
    gather x6 -> x0, local copies, waits for them, and re-layouts: 17.1 us -> none  [the longest x2 6.43 us: spread(): blocks = extended.reshape(-1, tile, width)[tile_cols]]
    unnamed x89 -> x3, local copies, waits for them, and re-layouts: 16.9 us -> 1.52 us
  transfers between devices with their start and end apart: 6 -> 1, of which waited for: 3 -> 1; matrix products, arithmetic and copies ran while one was open for 27% -> 1% of each run, Pallas kernels for 0% -> 0%
where the time goes in v1:
time: 140 us; the launch traced here: 139 us
  Pallas kernels  66.3 us (47%)
  blocking collectives  50.8 us (36%)
  waiting for transfers between devices  11.1 us (8%)
  starting transfers between devices  3.82 us (3%)
  other arithmetic  3.8 us (3%)
  local copies, waits for them, and re-layouts  2.25 us (2%)
    pallas_call x5, Pallas kernels, call(): pl.pallas_call(functools.partial(body, dims), in_specs=[sm] * smem + [vm]...  66.3 us
    all_to_all x3, blocking collectives, exchange(): lax.all_to_all(parcel, ('px', 'py'), split_axis=0, concat_axis=0, tiled=T...  50.8 us
    all_to_all x1, waiting for transfers between devices, exchange(): lax.all_to_all(parcel, ('px', 'py'), split_axis=0, concat_axis=0, tiled=T...  11.1 us
    all_to_all x1, starting transfers between devices, exchange(): lax.all_to_all(parcel, ('px', 'py'), split_axis=0, concat_axis=0, tiled=T...  3.82 us
  transfers between devices with their start and end apart: 1, of which 1 were waited for; matrix products, arithmetic and copies ran while one was open for 1% of the time, Pallas kernels for 0%

profile of v1, /device:TPU:0, one launch (start us, length us, event | category | flops | bytes accessed | tf_op | source)
XLA Modules:
  0.0 138.8 jit_solution(8778754535186009311)
XLA Ops:
  0.6 0.7 iota_compare_fusion
  1.4 0.8 copy.18
  2.1 0.2 lt.41
  2.3 0.9 broadcast_multiply_fusion
  3.3 0.1 copy.21
  3.4 0.1 copy.22
  3.5 0.2 squeeze.11
  3.7 0.8 compare_select_fusion.omega
  4.5 0.7 broadcast_select_fusion.idx
  5.2 11.0 %keys.1 = (bf16[2048,256]{1,0:T(8,128)(2,1)}, bf16[32,24,256]{2,1,0:T(8,128)(2,1)}) custom-call(s32[512,1]{1,0:T(8,128)} %broadcast_select_fusion.idx, bf16[2048,256]{1,0:T(8,128)(2,1)} %nodes.5, bf16[256,256]{1,0:T(8,128)(2,1)} %w_key.3, bf16[256,256]{1,0:T(8,128)(2,1)} %w_value.3, f32[256,256]{1,0:T(8,128)} %compare_select_fusion.omega), custom_call_target="tpu_custom_call" | custom-call | tf_op jit(solution)/shard_map/keys/pallas_call | solution.py:335
  16.2 19.3 %all_to_all.20.rec = bf16[32,24,256]{2,1,0:T(8,128)(2,1)} all-to-all(bf16[32,24,256]{2,1,0:T(8,128)(2,1)} %get-tuple-element.15), channel_id=1, replica_groups=mesh['px'=8,'py'=4] {'px','py'}, dimensions={0} | all-to-all | bytes 786432 | tf_op jit(solution)/shard_map/all_to_all | solution.py:346
  35.5 5.4 %near.1 = (bf16[2048,256]{1,0:T(8,128)(2,1)}, bf16[32,24,256]{2,1,0:T(8,128)(2,1)}, f32[8,256]{1,0:T(8,128)}) custom-call(s32[1,20]{1,0:T(1,128)} %row.5, s32[1,20]{1,0:T(1,128)} %col.5, s32[512,1]{1,0:T(8,128)} %broadcast_select_fusion.idx, bf16[2048,256]{1,0:T(8,128)(2,1)} %get-tuple-element.14.values_b, bf16[32,24,256]{2,1,0:T(8,128)(2,1)} %all_to_all.20.rec, ...), custom_call_target="tpu_custom_call" | custom-call | tf_op jit(solution)/shard_map/near/pallas_call | solution.py:335
  40.9 15.8 %all_to_all.21.rec = bf16[32,24,256]{2,1,0:T(8,128)(2,1)} all-to-all(bf16[32,24,256]{2,1,0:T(8,128)(2,1)} %get-tuple-element.17), channel_id=1, replica_groups=mesh['px'=8,'py'=4] {'px','py'}, dimensions={0} | all-to-all | bytes 786432 | tf_op jit(solution)/shard_map/all_to_all | solution.py:346
  56.7 26.7 %middle.1 = (bf16[2048,256]{1,0:T(8,128)(2,1)}, f32[2048,256]{1,0:T(8,128)}, f32[2048,256]{1,0:T(8,128)}, bf16[32,24,256]{2,1,0:T(8,128)(2,1)}) custom-call(s32[1,20]{1,0:T(1,128)} %row.5, s32[1,20]{1,0:T(1,128)} %col.5, f32[2,4]{1,0:T(2,128)} %coef.1, bf16[2048,256]{1,0:T(8,128)(2,1)} %nodes.5, bf16[2048,256]{1,0:T(8,128)(2,1)} %grad_out.1, ...), custom_call_target="tpu_custom_call" | custom-call | tf_op jit(solution)/shard_map/middle/pallas_call | solution.py:335
  83.4 3.8 %all-to-all-start.2 = ((bf16[32,24,256]{2,1,0:T(8,128)(2,1)}), bf16[32,24,256]{2,1,0:T(8,128)(2,1)S(1)}, u32[]{:S(2)}, u32[]{:S(2)}) async-start(bf16[32,24,256]{2,1,0:T(8,128)(2,1)} %get-tuple-element.22), calls=%async_computation.2 | async-start | bytes 786432 | tf_op jit(solution)/shard_map/all_to_all | solution.py:346
  87.2 0.1 lt.40
  87.3 0.1 squeeze.10
  87.3 0.6 broadcast_select_fusion.1.idx_row
  88.0 11.1 %all-to-all-done.2.rec = bf16[32,24,256]{2,1,0:T(8,128)(2,1)S(1)} async-done(((bf16[32,24,256]{2,1,0:T(8,128)(2,1)}), bf16[32,24,256]{2,1,0:T(8,128)(2,1)S(1)}, u32[]{:S(2)}, u32[]{:S(2)}) %all-to-all-start.2) | async-done | bytes 393248 | tf_op jit(solution)/shard_map/all_to_all | solution.py:346
  99.0 0.0 copy-start
  99.0 0.7 copy-done
  99.8 9.3 %back.1 = (f32[2048,256]{1,0:T(8,128)}, bf16[32,24,256]{2,1,0:T(8,128)(2,1)}, f32[8,256]{1,0:T(8,128)}) custom-call(s32[1,20]{1,0:T(1,128)} %row.5, s32[1,20]{1,0:T(1,128)} %col.5, s32[1,512]{1,0:T(1,128)} %broadcast_select_fusion.1.idx_row, f32[2048,256]{1,0:T(8,128)} %get-tuple-element.21.grad_near, bf16[32,24,256]{2,1,0:T(8,128)(2,1)} %copy-done, ...), custom_call_target="tpu_custom_call" | custom-call | tf_op jit(solution)/shard_map/back/pallas_call | solution.py:335
  109.1 15.8 %all_to_all.22.rec = bf16[32,24,256]{2,1,0:T(8,128)(2,1)} all-to-all(bf16[32,24,256]{2,1,0:T(8,128)(2,1)} %get-tuple-element.24), channel_id=1, replica_groups=mesh['px'=8,'py'=4] {'px','py'}, dimensions={0} | all-to-all | bytes 786432 | tf_op jit(solution)/shard_map/all_to_all | solution.py:346
  124.9 13.9 %last.1 = bf16[2048,256]{1,0:T(8,128)(2,1)} custom-call(s32[1,512]{1,0:T(1,128)} %broadcast_select_fusion.1.idx_row, bf16[2048,256]{1,0:T(8,128)(2,1)} %nodes.5, f32[2048,256]{1,0:T(8,128)} %get-tuple-element.20.partial, f32[2048,256]{1,0:T(8,128)} %get-tuple-element.23.grad_hop, bf16[32,24,256]{2,1,0:T(8,128)(2,1)} %all_to_all.22.rec, ...), custom_call_target="tpu_custom_call" | custom-call | tf_op jit(solution)/shard_map/last/pallas_call | solution.py:335
  (2 shorter events, 0.0 us)
Async XLA Ops:
  83.4 15.7 %all-to-all-start.2 = ((bf16[32,24,256]{2,1,0:T(8,128)(2,1)}), bf16[32,24,256]{2,1,0:T(8,128)(2,1)S(1)}, u32[]{:S(2)}, u32[]{:S(2)}) async-start(bf16[32,24,256]{2,1,0:T(8,128)(2,1)} %get-tuple-element.22), calls=%async_computation.2 | async-start | bytes 786432 | tf_op jit(solution)/shard_map/all_to_all | solution.py:346
  99.0 0.7 copy-start
